TPU v7x, 512 devices: a whole 4x4x16 slice. The times are simulated.
512 devices in a mesh: grp: 16 (over y, z_lo), blk: 32 (over x, z_hi, core).
Axes of the slice: x: 4, y: 4, z: 16 (z_hi: 4, z_lo: 4; z = z_hi * 4 + z_lo), core: 2. Of those that a mesh axis runs over, the one named last changes fastest.
Arguments:
- data: bfloat16 [1024, 65536], P('blk'), may hold values from -8 to 8
- labels: int32 [1024], P('blk'), may hold values from -1 to 1, as said below
- order: int32 [32, 4], P('blk'), may hold values from 0 to 3, each once within a row
- reg_index: int32 [16], P('grp'), parts along dimension 0, may hold values from 0 to 5
Outputs:
- dual: float32 [16384], P(('grp', 'blk')), parts along dimension 0
- margins: float32 [16384], P(('grp', 'blk')), parts along dimension 0
- gap: float32 [16], P('grp'), parts along dimension 0
There are 16 independent parts, one for each index of `grp`. A program takes and returns all parts, laid end to end along the dimension named above; an argument that names none is the same for every part. Nothing has to cross between parts.
Inputs may be any that keep to these rules, and one draw needn't show every extreme that they name: `labels`: each entry is -1 or 1.
All inputs are finite; a program needn't handle non-finite values.
Results may differ from a plain program's by a relative error of at most 0.00055.
Values sent between devices are 32-bit elements; how exact they have to be, the bound alone decides.
A program may use at most 64 MiB of HBM per device.

v0:
```python
import math

import jax
import jax.numpy as jnp
from jax import lax
from jax.sharding import PartitionSpec as P

NBLOCKS = 4
ROUNDS = 2


def in_blocks(x, dim, peers):
    shape = x.shape
    blocks = x.reshape(*shape[:dim], peers, shape[dim] // peers, *shape[dim + 1 :])
    return jnp.moveaxis(blocks, dim, 0)


def summed_on_arrival(x, axis, dim):
    peers = lax.axis_size(axis)
    blocks = lax.all_to_all(in_blocks(x, dim, peers), axis, 0, 0, tiled=True)
    return jnp.sum(blocks, axis=0)


def sent_to_all(x, axis):
    peers = lax.axis_size(axis)
    return lax.all_to_all(jnp.broadcast_to(x[None], (peers, *x.shape)), axis, 0, 0, tiled=True)


def joined_along(blocks, dim):
    blocks = jnp.moveaxis(blocks, 0, dim)
    shape = blocks.shape
    return blocks.reshape(*shape[:dim], shape[dim] * shape[dim + 1], *shape[dim + 2 :])


def collect(x, axis, dim):
    blocks = sent_to_all(x, axis)
    return joined_along(blocks, dim)


def of_everyone(x, axis):
    return sent_to_all(x, axis).sum(axis=0)


def together(arrays, axis):
    ends = [0]
    for a in arrays:
        ends.append(ends[-1] + a.size)
    subtotal = of_everyone(jnp.concatenate([a.ravel() for a in arrays]), axis)
    return tuple((subtotal[b:e].reshape(a.shape) for a, b, e in zip(arrays, ends, ends[1:])))


def local_round(shard_data, signs, dual, order_row, weights, reg_total, sigma_prime, squared):
    block_rows = shard_data.shape[0] // NBLOCKS
    feature_scale = 1.0 / math.sqrt(shard_data.shape[1])
    local_weights = weights
    dual_change = jnp.zeros_like(dual)
    for position in range(NBLOCKS):
        offset = order_row[position] * block_rows
        block_data = lax.dynamic_slice_in_dim(shard_data, offset, block_rows, 0)
        block_signs = lax.dynamic_slice_in_dim(signs, offset, block_rows, 0)
        block_dual = lax.dynamic_slice_in_dim(dual, offset, block_rows, 0)
        block_change = lax.dynamic_slice_in_dim(dual_change, offset, block_rows, 0)
        block_norms = lax.dynamic_slice_in_dim(squared, offset, block_rows, 0)
        rounded = local_weights.astype(jnp.bfloat16)
        score = feature_scale * jnp.dot(block_data, rounded, preferred_element_type=jnp.float32)
        current = block_dual + block_change
        updated = jnp.clip(
            current + reg_total * (1.0 - block_signs * score) / (sigma_prime * block_norms),
            0.0,
            1.0,
        )
        change = updated - current
        dual_change = lax.dynamic_update_slice_in_dim(dual_change, block_change + change, offset, 0)
        coefficient = (block_signs * change).astype(jnp.bfloat16)
        local_weights = local_weights + sigma_prime * feature_scale / reg_total * jnp.dot(
            coefficient, block_data, preferred_element_type=jnp.float32
        )
    return dual_change


def shards(data, labels, order, reg_index):
    group_size = lax.axis_size("blk")
    row_count = data.shape[0]
    feature_count = data.shape[1]
    samples_all = row_count * group_size
    feature_scale = 1.0 / math.sqrt(feature_count)
    reg_strength = 0.04 * jnp.exp(0.5 * math.log(2.0) * reg_index[0].astype(jnp.float32))
    reg_total = reg_strength * samples_all
    sigma_prime = jnp.float32(group_size)
    signs = labels.astype(jnp.float32)
    squared = (
        jnp.einsum("rf,rf->r", data, data, preferred_element_type=jnp.float32) / feature_count
        + 1e-06
    )
    weights = jnp.zeros((feature_count,), jnp.float32)
    dual = jnp.zeros((row_count,), jnp.float32)
    for round_index in range(ROUNDS):
        dual_change = local_round(
            data, signs, dual, order[0], weights, reg_total, sigma_prime, squared
        )
        coefficient = (signs * dual_change).astype(jnp.bfloat16)
        delta = (
            feature_scale
            / reg_total
            * jnp.dot(coefficient, data, preferred_element_type=jnp.float32)
        )
        share = feature_count // group_size
        summed = summed_on_arrival(delta, "blk", 0)
        own_part = lax.dynamic_slice_in_dim(weights, lax.axis_index("blk") * share, share, 0)
        weights = collect(own_part + summed, "blk", 0)
        dual = dual + dual_change
    margins = feature_scale * jnp.dot(
        data, weights.astype(jnp.bfloat16), preferred_element_type=jnp.float32
    )
    hinge = jnp.maximum(0.0, 1.0 - signs * margins)
    hinge_total, dual_total = together((jnp.sum(hinge), jnp.sum(dual)), "blk")
    gap = reg_strength * jnp.sum(weights * weights) + (hinge_total - dual_total) / samples_all
    return (dual, margins, gap.reshape(1))


def solution(mesh):
    placed = (P("blk", None), P("blk"), P("blk", None), P("grp"))
    return jax.shard_map(
        shards,
        mesh=mesh,
        in_specs=placed,
        out_specs=(P(("grp", "blk")), P(("grp", "blk")), P("grp")),
        check_vma=False,
    )
```

profile of v0, /device:TPU:1, one launch (start us, length us, event | category | flops | bytes accessed | tf_op | source)
XLA Modules:
  0.0 191.1 jit_solution(15073682413429723824)
XLA Ops:
  0.6 1.5 fusion.135
  4.1 0.7 convert_element_type.62
  4.8 3.1 %fusion = f32[32]{0:T(128)S(1)} fusion(bf16[32,65536]{1,0:T(8,128)(2,1)} %param.4), kind=kLoop, calls=%fused_computation.1 | loop fusion | flops 6291424 | bytes 4194432 | tf_op jit(solution)/shard_map/rf,rf->r/dot_general | solution.py:92
  8.7 2.1 %fusion.6 = f32[8]{0:T(128)S(1)} fusion(f32[8]{0:T(128)S(1)} %get-tuple-element.15, bf16[32,65536]{1,0:T(8,128)(2,1)} %param.4, s32[]{:T(128)S(6)} %select_n.10, f32[32]{0:T(128)S(1)} %multiply_add_fusion.3, f32[]{:T(128)} %bitcast), kind=kOutput, calls=%fused_computation.15 | convolution fusion | flops 1048632 | bytes 1050208 | tf_op jit(solution)/shard_map/dot_general | solution.py:65
  10.7 1.7 fusion.83
  12.9 2.2 %fusion.14 = f32[8]{0:T(128)S(1)} fusion(f32[8]{0:T(128)S(1)} %get-tuple-element.14, bf16[65536,1]{0,1:T(2,128)(2,1)S(1)} %reshape.88, bf16[32,65536]{1,0:T(8,128)(2,1)} %param.4, s32[]{:T(128)S(6)} %select_n.11, f32[32]{0:T(128)S(1)} %multiply_add_fusion.3, f32[]{:T(128)} %bitcast, f32[32]{0:T(128)S(1)} %dynamic_update_slice.24), kind=kOutput, calls=%fused_computation.23 | convolution fusion | flops 1048648 | bytes 1181312 | tf_op jit(solution)/shard_map/dot_general | solution.py:65
  15.3 1.6 fusion.77
  17.1 0.9 fusion.22
  19.4 2.1 %fusion.31 = f32[8]{0:T(128)S(1)} fusion(bf16[65536,1]{0,1:T(2,128)(2,1)S(1)} %reshape.96, bf16[32,65536]{1,0:T(8,128)(2,1)} %param.4, s32[]{:T(128)S(6)} %select_n.13, f32[32]{0:T(128)S(1)} %add_dynamic-update-slice_fusion.2, f32[32]{0:T(128)S(1)} %multiply_add_fusion.3, f32[]{:T(128)} %bitcast, f32[32]{0:T(128)S(1)} %convert_element_type.62), kind=kOutput, calls=%fused_computation.40 | convolution fusion | flops 1048656 | bytes 1181312 | tf_op jit(solution)/shard_map/dot_general | solution.py:65
  21.7 2.8 %fusion.108 = f32[1,65536]{1,0:T(1,128)S(1)} fusion(bf16[32,65536]{1,0:T(8,128)(2,1)} %param.4, f32[32]{0:T(128)S(1)} %dynamic_update_slice.27, s32[32]{0:T(128)S(1)} %copy-done.2), kind=kOutput, calls=%fused_computation.129 | convolution fusion | flops 4194400 | bytes 4456704 | tf_op jit(solution)/shard_map/dot_general | solution.py:105
  24.7 39.2 %all_to_all.37 = f32[32,1,2048]{2,1,0:T(1,128)S(1)} all-to-all(f32[32,1,2048]{2,1,0:T(1,128)S(1)} %bitcast.222), channel_id=1, replica_groups=mesh['grp'=16,'blk'=32] {'blk'}, dimensions={0} | all-to-all | bytes 524288 | tf_op jit(solution)/shard_map/all_to_all | solution.py:20
  64.2 26.2 %all_to_all.36 = f32[32,1,2048]{2,1,0:T(1,128)S(1)} all-to-all(f32[32,1,2048]{2,1,0:T(1,128)S(1)} %broadcast_in_dim.6), channel_id=1, replica_groups=mesh['grp'=16,'blk'=32] {'blk'}, dimensions={0} | all-to-all | bytes 524288 | tf_op jit(solution)/shard_map/all_to_all | solution.py:26
  90.5 2.1 %fusion.39 = f32[8]{0:T(128)S(1)} fusion(f32[8]{0:T(128)S(1)} %get-tuple-element.15, bf16[65536,1]{0,1:T(2,128)(2,1)S(1)} %reshape.100, bf16[32,65536]{1,0:T(8,128)(2,1)} %param.4, s32[]{:T(128)S(6)} %select_n.10, f32[32]{0:T(128)S(1)} %dynamic_update_slice.27, f32[32]{0:T(128)S(1)} %multiply_add_fusion.3, f32[]{:T(128)} %bitcast), kind=kOutput, calls=%fused_computation.48 | convolution fusion | flops 1048648 | bytes 1181312 | tf_op jit(solution)/shard_map/dot_general | solution.py:65
  92.6 1.7 fusion.80
  94.7 2.2 %fusion.47 = f32[8]{0:T(128)S(1)} fusion(f32[8]{0:T(128)S(1)} %get-tuple-element.14, bf16[65536,1]{0,1:T(2,128)(2,1)S(1)} %reshape.104, bf16[32,65536]{1,0:T(8,128)(2,1)} %param.4, s32[]{:T(128)S(6)} %select_n.11, f32[32]{0:T(128)S(1)} %dynamic_update_slice.27, f32[32]{0:T(128)S(1)} %multiply_add_fusion.3, f32[]{:T(128)} %bitcast, ...), kind=kOutput, calls=%fused_computation.56 | convolution fusion | flops 1048656 | bytes 1181344 | tf_op jit(solution)/shard_map/dot_general | solution.py:65
  97.1 1.6 fusion.74
  98.9 0.9 fusion.55
  100.7 0.9 fusion.64
  101.7 2.8 %fusion.103 = f32[1,65536]{1,0:T(1,128)S(1)} fusion(bf16[32,65536]{1,0:T(8,128)(2,1)} %param.4, f32[32]{0:T(128)S(1)} %dynamic_update_slice.31, s32[32]{0:T(128)S(1)} %copy-done.2), kind=kOutput, calls=%fused_computation.124 | convolution fusion | flops 4194400 | bytes 4456704 | tf_op jit(solution)/shard_map/dot_general | solution.py:105
  104.6 0.7 broadcast_multiply_fusion
  105.3 6.0 %all-to-all-start.2 = ((f32[32,1,2048]{2,1,0:T(1,128)}), f32[32,1,2048]{2,1,0:T(1,128)S(1)}, u32[]{:S(2)}, u32[]{:S(2)}) async-start(f32[32,1,2048]{2,1,0:T(1,128)} %bitcast.31), calls=%async_computation.2 | async-start | bytes 524288 | tf_op jit(solution)/shard_map/all_to_all | solution.py:20
  111.3 20.2 %all-to-all-done.2 = f32[32,1,2048]{2,1,0:T(1,128)S(1)} async-done(((f32[32,1,2048]{2,1,0:T(1,128)}), f32[32,1,2048]{2,1,0:T(1,128)S(1)}, u32[]{:S(2)}, u32[]{:S(2)}) %all-to-all-start.2) | async-done | bytes 262176 | tf_op jit(solution)/shard_map/all_to_all | solution.py:20
  131.7 0.8 broadcast_in_dim.7
  132.5 6.7 %all-to-all-start.3 = ((f32[32,1,2048]{2,1,0:T(1,128)}), f32[32,1,2048]{2,1,0:T(1,128)S(1)}, u32[]{:S(2)}, u32[]{:S(2)}) async-start(f32[32,1,2048]{2,1,0:T(1,128)} %broadcast_in_dim.7), calls=%async_computation.3 | async-start | bytes 524288 | tf_op jit(solution)/shard_map/all_to_all | solution.py:26
  139.2 1.1 fusion.133
  140.3 19.1 %all-to-all-done.3 = f32[32,1,2048]{2,1,0:T(1,128)S(1)} async-done(((f32[32,1,2048]{2,1,0:T(1,128)}), f32[32,1,2048]{2,1,0:T(1,128)S(1)}, u32[]{:S(2)}, u32[]{:S(2)}) %all-to-all-start.3) | async-done | bytes 262176 | tf_op jit(solution)/shard_map/all_to_all | solution.py:26
  159.4 1.1 multiply_reduce_fusion
  160.5 4.6 %maximum_reduce_fusion = (f32[]{:T(128)}, f32[32]{0:T(128)}) fusion(s32[32]{0:T(128)S(1)} %copy-done.2, bf16[65536,1]{0,1:T(2,128)(2,1)S(1)} %bitcast.225, bf16[32,65536]{1,0:T(8,128)(2,1)} %param.4), kind=kOutput, calls=%fused_computation.134 | convolution fusion | flops 4194495 | bytes 4325636 | tf_op jit(solution)/shard_map/dot_general | solution.py:112
  165.1 1.4 pad_maximum_fusion
  166.5 0.6 broadcast_in_dim.8
  167.1 6.7 %all-to-all-start.4 = ((f32[32,1,2]{2,1,0:T(1,128)}), f32[32,1,2]{2,1,0:T(1,128)S(1)}, u32[]{:S(2)}, u32[]{:S(2)}) async-start(f32[32,1,2]{2,1,0:T(1,128)} %broadcast_in_dim.8), calls=%async_computation.4 | async-start | bytes 32768 | tf_op jit(solution)/shard_map/all_to_all | solution.py:26
  174.4 13.7 %all-to-all-done.4 = f32[32,1,2]{2,1,0:T(1,128)S(1)} async-done(((f32[32,1,2]{2,1,0:T(1,128)}), f32[32,1,2]{2,1,0:T(1,128)S(1)}, u32[]{:S(2)}, u32[]{:S(2)}) %all-to-all-start.4) | async-done | bytes 288 | tf_op jit(solution)/shard_map/all_to_all | solution.py:26
  (41 shorter events, 4.9 us)
Async XLA Ops:
  12.7 4.4 %copy-start = (bf16[32,65536]{1,0:T(8,128)(2,1)S(1)}, bf16[32,65536]{1,0:T(8,128)(2,1)}, u32[]{:S(2)}) copy-start(bf16[32,65536]{1,0:T(8,128)(2,1)} %param.4) | copy-start | bytes 12582916
  15.1 6.6 %copy-start.2 = (s32[32]{0:T(128)S(1)}, s32[32]{0:T(128)}, u32[]{:S(2)}) copy-start(s32[32]{0:T(128)} %param.5) | copy-start | bytes 388
  94.5 4.4 %copy-start.1 = (bf16[32,65536]{1,0:T(8,128)(2,1)S(1)}, bf16[32,65536]{1,0:T(8,128)(2,1)}, u32[]{:S(2)}) copy-start(bf16[32,65536]{1,0:T(8,128)(2,1)} %param.4) | copy-start | bytes 12582916
  105.3 26.2 %all-to-all-start.2 = ((f32[32,1,2048]{2,1,0:T(1,128)}), f32[32,1,2048]{2,1,0:T(1,128)S(1)}, u32[]{:S(2)}, u32[]{:S(2)}) async-start(f32[32,1,2048]{2,1,0:T(1,128)} %bitcast.31), calls=%async_computation.2 | async-start | bytes 524288 | tf_op jit(solution)/shard_map/all_to_all | solution.py:20
  132.5 26.9 %all-to-all-start.3 = ((f32[32,1,2048]{2,1,0:T(1,128)}), f32[32,1,2048]{2,1,0:T(1,128)S(1)}, u32[]{:S(2)}, u32[]{:S(2)}) async-start(f32[32,1,2048]{2,1,0:T(1,128)} %broadcast_in_dim.7), calls=%async_computation.3 | async-start | bytes 524288 | tf_op jit(solution)/shard_map/all_to_all | solution.py:26
  167.1 20.9 %all-to-all-start.4 = ((f32[32,1,2]{2,1,0:T(1,128)}), f32[32,1,2]{2,1,0:T(1,128)S(1)}, u32[]{:S(2)}, u32[]{:S(2)}) async-start(f32[32,1,2]{2,1,0:T(1,128)} %broadcast_in_dim.8), calls=%async_computation.4 | async-start | bytes 32768 | tf_op jit(solution)/shard_map/all_to_all | solution.py:26
where the time goes:
time: 192 us; the launch traced here: 191 us
  blocking collectives  65.4 us (34%)
  waiting for transfers between devices  53 us (28%)
  matrix products  31 us (16%)
  starting transfers between devices  19.3 us (10%)
  other arithmetic  9.49 us (5%)
  between operations  7.39 us (4%)
  local copies, waits for them, and re-layouts  5.6 us (3%)
    all_to_all x1, blocking collectives, summed_on_arrival(): blocks = lax.all_to_all(in_blocks(x, dim, peers), axis, 0, 0, tiled=True)  39.2 us
    all_to_all x2, waiting for transfers between devices, sent_to_all(): lax.all_to_all(jnp.broadcast_to(x[None], (peers, *x.shape)), axis, 0, 0,...  32.8 us
    all_to_all x1, blocking collectives, sent_to_all(): lax.all_to_all(jnp.broadcast_to(x[None], (peers, *x.shape)), axis, 0, 0,...  26.2 us
    all_to_all x1, waiting for transfers between devices, summed_on_arrival(): blocks = lax.all_to_all(in_blocks(x, dim, peers), axis, 0, 0, tiled=True)  20.2 us
    all_to_all x2, starting transfers between devices, sent_to_all(): lax.all_to_all(jnp.broadcast_to(x[None], (peers, *x.shape)), axis, 0, 0,...  13.3 us
    dot_general x8, matrix products, local_round(): jnp.dot(block_data, rounded, preferred_element_type=jnp.float32)  13.2 us
    dot_general x6, matrix products, local_round(): jnp.dot(coefficient, block_data, preferred_element_type=jnp.float32)  7.46 us
    all_to_all x1, starting transfers between devices, summed_on_arrival(): blocks = lax.all_to_all(in_blocks(x, dim, peers), axis, 0, 0, tiled=True)  5.99 us
  transfers between devices with their start and end apart: 3, of which 3 were waited for; matrix products, arithmetic and copies ran while one was open for 1% of the time, Pallas kernels for 0%

commit v1 on v0

v1 whole, which is shorter than its diff:
```python
import functools
import math

import jax
import jax.numpy as jnp
from jax import lax
from jax.experimental import pallas as pl
from jax.experimental.pallas import tpu as pltpu
from jax.sharding import PartitionSpec as P

NBLOCKS = 4
ROUNDS = 2
REGS = 6
Y, ZLO = 4, 4
X, ZHI, CORE = 4, 4, 2
PLANE = X * CORE
GRP = Y * ZLO
LANES = 128
MESH = pl.DeviceIdType.MESH


def kernel(
    samples_all,
    chunks,
    labels_ref,
    order_ref,
    reg_ref,
    data_hbm,
    dual_out,
    margins_out,
    gap_out,
    data,
    load_sem,
    delta,
    sums1,
    part2,
    sums2,
    own3,
    weights,
    sums4,
    local5,
    sums5,
    local6,
    sums6,
    plane_send,
    plane_recv,
    cube_send,
    cube_recv,
    grp_send,
    grp_recv,
):
    rows, features = data.shape
    share = features // GRP
    piece = share // PLANE
    grp, blk = lax.axis_index("grp"), lax.axis_index("blk")
    y, zlo = grp // ZLO, lax.rem(grp, ZLO)
    x, zhi, core = blk // (ZHI * CORE), lax.rem(blk // CORE, ZHI), lax.rem(blk, CORE)
    part = lax.rem(zlo + 2 * (zhi // 2), ZLO)
    mine = x * CORE + core

    def plane_peer(d):
        other = lax.rem(mine + d, PLANE)
        return other, (grp, (other // CORE) * ZHI * CORE + zhi * CORE + lax.rem(other, CORE))

    def cube_peer(d):
        other = lax.rem(zhi + d, ZHI)
        other_zlo = lax.rem(part + 2 * (other // 2), ZLO)
        return (y * ZLO + other_zlo, x * ZHI * CORE + other * CORE + core)

    def grp_peer(d):
        return (lax.rem(grp + d, GRP), blk)

    peers = [plane_peer(d)[1] for d in range(1, PLANE)]
    peers += [cube_peer(d) for d in range(1, ZHI)]
    peers += [grp_peer(d) for d in range(1, GRP)]

    width = features // chunks
    loads = [
        pltpu.make_async_copy(
            data_hbm.at[:, pl.ds(i * width, width)],
            data.at[:, pl.ds(i * width, width)],
            load_sem.at[i],
        )
        for i in range(chunks)
    ]
    for load in loads:
        load.start()
    barrier = pltpu.get_barrier_semaphore()
    for peer in peers:
        pl.semaphore_signal(barrier, inc=1, device_id=peer, device_id_type=MESH)

    contract_last = (((1,), (1,)), ((), ()))
    gram = jnp.zeros((rows, rows), jnp.float32)
    for i, load in enumerate(loads):
        load.wait()
        block = data[:, pl.ds(i * width, width)]
        gram = gram + lax.dot_general(
            block, block, contract_last, preferred_element_type=jnp.float32
        )

    scale = 1.0 / math.sqrt(features)
    sigma = float(X * ZHI * CORE)
    reg_row = lax.broadcasted_iota(jnp.int32, (REGS, 1), 0)
    strength = 0.04 * jnp.exp(0.5 * math.log(2.0) * reg_row.astype(jnp.float32))
    total = strength * samples_all
    row = lax.broadcasted_iota(jnp.int32, (rows, rows), 0)
    col = lax.broadcasted_iota(jnp.int32, (rows, rows), 1)
    squared = jnp.sum(jnp.where(row == col, gram, 0.0), axis=0, keepdims=True) / features + 1e-6
    high = gram.astype(jnp.bfloat16)
    low = (gram - high.astype(jnp.float32)).astype(jnp.bfloat16)
    signs = labels_ref[...].astype(jnp.float32)
    block_of = lax.broadcasted_iota(jnp.int32, (1, rows), 1) // (rows // NBLOCKS)
    visits = [block_of == order_ref[0, t] for t in range(NBLOCKS)]
    gain = total / (sigma * squared)
    coupling = sigma * scale * scale / total

    def local_round(base, dual):
        full = jnp.zeros((REGS, rows), jnp.float32)
        new_dual = dual
        for t in range(NBLOCKS):
            score = base
            if t:
                coef = full.astype(jnp.bfloat16)
                score = base + coupling * (
                    jnp.dot(coef, high, preferred_element_type=jnp.float32)
                    + jnp.dot(coef, low, preferred_element_type=jnp.float32)
                )
            updated = jnp.clip(dual + gain * (1.0 - signs * score), 0.0, 1.0)
            step = (signs * (updated - dual)).astype(jnp.bfloat16).astype(jnp.float32)
            full = jnp.where(visits[t], step, full)
            new_dual = jnp.where(visits[t], updated, new_dual)
        return full, new_dual

    dual = jnp.zeros((REGS, rows), jnp.float32)
    full, dual = local_round(jnp.zeros((REGS, rows), jnp.float32), dual)
    pl.semaphore_wait(barrier, len(peers))

    def copy(source, target, sends, recvs, i, peer):
        return pltpu.make_async_remote_copy(
            src_ref=source,
            dst_ref=target,
            send_sem=sends.at[i],
            recv_sem=recvs.at[i],
            device_id=peer,
            device_id_type=MESH,
        )

    pending = []

    def to_plane(stage, make):
        copies = []
        for d in range(1, PLANE):
            other, peer = plane_peer(d)
            source, target = make(d, other)
            c = copy(source, target, plane_send, plane_recv, stage * (PLANE - 1) + d - 1, peer)
            c.start()
            copies.append(c)
        pending.extend(copies)
        return copies

    def to_cubes(stage, source, target):
        copies = []
        for d in range(1, ZHI):
            c = copy(source, target, cube_send, cube_recv, stage * (ZHI - 1) + d - 1, cube_peer(d))
            c.start()
            copies.append(c)
        pending.extend(copies)
        return copies

    def to_grp(stage, source, target):
        copies = []
        for d in range(1, GRP):
            c = copy(source, target, grp_send, grp_recv, stage * (GRP - 1) + d - 1, grp_peer(d))
            c.start()
            copies.append(c)
        pending.extend(copies)
        return copies

    def arrived(copies):
        for c in copies:
            c.wait_recv()

    start = pl.multiple_of((y * ZLO + part) * share, share)
    own = pl.ds(pl.multiple_of(mine * piece, piece), piece)
    held = None
    for r in range(ROUNDS):
        delta[r] = (scale / total) * jnp.dot(
            full.astype(jnp.bfloat16),
            data[:, pl.ds(start, share)],
            preferred_element_type=jnp.float32,
        )

        def scatter(d, other):
            where = pl.ds(pl.multiple_of(other * piece, piece), piece)
            return delta.at[r, :, where], sums1.at[r, d - 1]

        arrived(to_plane(2 * r, scatter))
        summed = delta[r, :, own]
        for d in range(1, PLANE):
            summed = summed + sums1[r, d - 1]

        part2[r] = summed
        sums2[r, zhi] = summed
        arrived(to_cubes(r, part2.at[r], sums2.at[r, zhi]))
        summed = sums2[r, 0]
        for h in range(1, ZHI):
            summed = summed + sums2[r, h]
        held = summed if held is None else held + summed

        own3[r] = held
        weights[r, mine] = held
        arrived(to_plane(2 * r + 1, lambda d, other: (own3.at[r], weights.at[r, mine])))
        score = jnp.zeros((REGS, rows), jnp.float32)
        norm = jnp.zeros((REGS, 1), jnp.float32)
        for j in range(PLANE):
            w = weights[r, j]
            score = score + lax.dot_general(
                w.astype(jnp.bfloat16),
                data[:, pl.ds(pl.multiple_of(start + j * piece, piece), piece)],
                contract_last,
                preferred_element_type=jnp.float32,
            )
            norm = norm + jnp.sum(w * w, axis=1, keepdims=True)
        tile = jnp.concatenate(
            [scale * score, jnp.broadcast_to(norm, (REGS, LANES - rows))], axis=1
        )

        own4 = local5.at[r]
        own4[...] = tile
        sums4[r, grp] = tile
        arrived(to_grp(r, own4, sums4.at[r, grp]))
        tile = sums4[r, 0]
        for j in range(1, GRP):
            tile = tile + sums4[r, j]
        margins, norm = tile[:, :rows], tile[:, rows : rows + 1]
        if r + 1 < ROUNDS:
            full, dual = local_round(margins, dual)

    chosen = reg_row == reg_ref[0]
    dual_out[...] = jnp.sum(jnp.where(chosen, dual, 0.0), axis=0, keepdims=True)
    margins_out[...] = jnp.sum(jnp.where(chosen, margins, 0.0), axis=0, keepdims=True)
    hinge = jnp.maximum(0.0, 1.0 - signs * margins)
    mine_total = jnp.broadcast_to(
        jnp.sum(hinge - dual, axis=1, keepdims=True), (REGS, LANES)
    )
    local6[0] = mine_total
    sums5[mine] = mine_total
    arrived(to_plane(2 * ROUNDS, lambda d, other: (local6.at[0], sums5.at[mine])))
    plane_total = sums5[0]
    for j in range(1, PLANE):
        plane_total = plane_total + sums5[j]
    local6[1] = plane_total
    sums6[zhi] = plane_total
    arrived(to_cubes(ROUNDS, local6.at[1], sums6.at[zhi]))
    all_total = sums6[0]
    for h in range(1, ZHI):
        all_total = all_total + sums6[h]
    gap = strength * norm + all_total[:, :1] / samples_all
    gap_out[...] = jnp.sum(jnp.where(chosen, gap, 0.0), axis=0, keepdims=True)
    for c in pending:
        c.wait_send()


def shards(data, labels, order, reg_index):
    rows, features = data.shape
    share = features // GRP
    piece = share // PLANE
    chunks = 8
    f32 = functools.partial(jax.ShapeDtypeStruct, dtype=jnp.float32)
    vmem = pl.BlockSpec(memory_space=pltpu.VMEM)
    smem = pl.BlockSpec(memory_space=pltpu.SMEM)
    scratch = lambda *shape: pltpu.VMEM(shape, jnp.float32)
    sems = lambda n: pltpu.SemaphoreType.DMA((n,))
    dual, margins, gap = pl.pallas_call(
        functools.partial(kernel, rows * lax.axis_size("blk"), chunks),
        out_shape=(f32((1, rows)), f32((1, rows)), f32((1, 1))),
        in_specs=[vmem, smem, smem, pl.BlockSpec(memory_space=pl.ANY)],
        out_specs=(vmem, vmem, vmem),
        scratch_shapes=[
            pltpu.VMEM((rows, features), jnp.bfloat16),
            sems(chunks),
            scratch(ROUNDS, REGS, share),
            scratch(ROUNDS, PLANE - 1, REGS, piece),
            scratch(ROUNDS, REGS, piece),
            scratch(ROUNDS, ZHI, REGS, piece),
            scratch(ROUNDS, REGS, piece),
            scratch(ROUNDS, PLANE, REGS, piece),
            scratch(ROUNDS, GRP, REGS, LANES),
            scratch(ROUNDS, REGS, LANES),
            scratch(PLANE, REGS, LANES),
            scratch(2, REGS, LANES),
            scratch(ZHI, REGS, LANES),
            sems((2 * ROUNDS + 1) * (PLANE - 1)),
            sems((2 * ROUNDS + 1) * (PLANE - 1)),
            sems((ROUNDS + 1) * (ZHI - 1)),
            sems((ROUNDS + 1) * (ZHI - 1)),
            sems(ROUNDS * (GRP - 1)),
            sems(ROUNDS * (GRP - 1)),
        ],
        compiler_params=pltpu.CompilerParams(collective_id=0, has_side_effects=True),
    )(labels.reshape(1, rows), order, reg_index, data)
    return dual.reshape(rows), margins.reshape(rows), gap.reshape(1)


def solution(mesh):
    placed = (P("blk", None), P("blk"), P("blk", None), P("grp"))
    return jax.shard_map(
        shards,
        mesh=mesh,
        in_specs=placed,
        out_specs=(P(("grp", "blk")), P(("grp", "blk")), P("grp")),
        check_vma=False,
    )
```

time: 192 us -> 74.5 us (0.39)
  Pallas kernels: 0 us -> 69 us
  blocking collectives: 65.4 us -> 0 us
  waiting for transfers between devices: 53 us -> 0 us
  matrix products: 31 us -> 0 us
  starting transfers between devices: 19.3 us -> 0 us
  other arithmetic: 9.49 us -> 0 us
  between operations: 7.39 us -> 3.05 us
  local copies, waits for them, and re-layouts: 5.6 us -> 2.25 us
    pallas_call x0 -> x1, Pallas kernels: none -> 69 us  [shards(): pl.pallas_call(functools.partial(kernel, rows * lax.axis_size('blk'), chu...]
    all_to_all x2 -> x0, blocking collectives: 65.4 us -> none  [the longest x1 39.2 us: summed_on_arrival(): blocks = lax.all_to_all(in_blocks(x, dim, peers), axis, 0, 0, tiled=True)]
    all_to_all x3 -> x0, waiting for transfers between devices: 53 us -> none  [the longest x2 32.8 us: sent_to_all(): lax.all_to_all(jnp.broadcast_to(x[None], (peers, *x.shape)), axis, 0, 0,...]
    dot_general x17 -> x0, matrix products: 31 us -> none  [the longest x8 13.2 us: local_round(): jnp.dot(block_data, rounded, preferred_element_type=jnp.float32)]
    all_to_all x3 -> x0, starting transfers between devices: 19.3 us -> none  [the longest x2 13.3 us: sent_to_all(): lax.all_to_all(jnp.broadcast_to(x[None], (peers, *x.shape)), axis, 0, 0,...]
    dot_general x1 -> x0, other arithmetic: 3.1 us -> none  [shards(): jnp.einsum('rf,rf->r', data, data, preferred_element_type=jnp.float32)]
    reduce_sum x5 -> x0, other arithmetic: 2.62 us -> none  [the longest x1 1.13 us: shards(): jnp.sum(weights * weights)]
    unnamed x6 -> x2, local copies, waits for them, and re-layouts: 0.01 us -> 2.25 us
  transfers between devices with their start and end apart: 3 -> 0, of which waited for: 3 -> 0; matrix products, arithmetic and copies ran while one was open for 1% -> 0% of each run, Pallas kernels for 0% -> 0%
where the time goes in v1:
time: 74.5 us; the launch traced here: 74.3 us
  Pallas kernels  69 us (93%)
  between operations  3.05 us (4%)
  local copies, waits for them, and re-layouts  2.25 us (3%)
    pallas_call x1, Pallas kernels, shards(): pl.pallas_call(functools.partial(kernel, rows * lax.axis_size('blk'), chu...  69 us
    unnamed x2, local copies, waits for them, and re-layouts  2.25 us

profile of v1, /device:TPU:1, one launch (start us, length us, event | category | flops | bytes accessed | tf_op | source)
XLA Modules:
  0.0 74.3 jit_solution(11640658393550954123)
XLA Ops:
  1.3 69.0 %shard_map.67 = (f32[1,32]{1,0:T(1,128)}, f32[1,32]{1,0:T(1,128)}, f32[1,1]{1,0:T(1,128)}) custom-call(s32[1,32]{1,0:T(1,128)} %bitcast.4, s32[1,4]{1,0:T(1,128)} %order_ref.1, s32[1]{0:T(128)S(6)} %copy.10.reg_ref, bf16[32,65536]{1,0:T(8,128)(2,1)} %data_hbm.1), custom_call_target="tpu_custom_call" | custom-call | tf_op jit(solution)/shard_map/pallas_call | solution.py:274
  70.3 1.1 %copy.11 = f32[32]{0:T(128)} copy(f32[32]{0:T(128)} %bitcast.6) | data formatting | bytes 256
  71.4 1.1 %copy.12 = f32[32]{0:T(128)} copy(f32[32]{0:T(128)} %bitcast.5) | data formatting | bytes 256

commit v2 on v1

v2 whole, which is shorter than its diff:
```python
import functools
import math

import jax
import jax.numpy as jnp
from jax import lax
from jax.experimental import pallas as pl
from jax.experimental.pallas import tpu as pltpu
from jax.sharding import PartitionSpec as P

NBLOCKS = 4
ROUNDS = 2
REGS = 6
Y, ZLO = 4, 4
X, ZHI, CORE = 4, 4, 2
PLANE = X * CORE
GRP = Y * ZLO
LANES = 128
REACH = 6
MESH = pl.DeviceIdType.MESH


def kernel(
    samples_all,
    chunks,
    labels_hbm,
    order_hbm,
    reg_hbm,
    data_hbm,
    out,
    labels_ref,
    order_ref,
    reg_ref,
    small_sem,
    data,
    load_sem,
    delta,
    sums1,
    part2,
    sums2,
    wide,
    across,
    facts_own,
    facts,
    local3,
    sums3,
    local4,
    sums4,
    last3,
    last_sums3,
    last4,
    last_sums4,
    local5,
    sums5,
    plane_send,
    plane_recv,
    cube_send,
    cube_recv,
    grp_send,
    grp_recv,
    relay,
):
    rows, features = data.shape
    share = features // GRP
    piece = share // PLANE
    wide_rows = PLANE * rows
    grp, blk = lax.axis_index("grp"), lax.axis_index("blk")
    y, zlo = grp // ZLO, lax.rem(grp, ZLO)
    x, zhi, core = blk // (ZHI * CORE), lax.rem(blk // CORE, ZHI), lax.rem(blk, CORE)
    part = lax.rem(zlo + 2 * (zhi // 2), ZLO)
    mine = x * CORE + core

    def plane_peer(d):
        other = lax.rem(mine + d, PLANE)
        return other, (grp, (other // CORE) * ZHI * CORE + zhi * CORE + lax.rem(other, CORE))

    def cube_peer(d):
        other = lax.rem(zhi + d, ZHI)
        other_zlo = lax.rem(part + 2 * (other // 2), ZLO)
        return (y * ZLO + other_zlo, x * ZHI * CORE + other * CORE + core)

    def grp_peer(d):
        return (lax.rem(grp + d, GRP), blk)

    def z_peer(d):
        z = lax.rem(zhi * ZLO + zlo + d + ZHI * ZLO, ZHI * ZLO)
        return (y * ZLO + lax.rem(z, ZLO), x * ZHI * CORE + (z // ZLO) * CORE + core)

    left, right = z_peer(-1), z_peer(1)
    peers = [plane_peer(d)[1] for d in range(1, PLANE)]
    peers += [(lax.rem(grp + d * ZLO, GRP), blk) for d in range(1, Y)]
    peers += [left, right]

    width = features // chunks
    loads = [
        pltpu.make_async_copy(
            data_hbm.at[:, pl.ds(i * width, width)],
            data.at[:, pl.ds(i * width, width)],
            load_sem.at[i],
        )
        for i in range(chunks)
    ]
    for load in loads:
        load.start()
    small = [
        pltpu.make_async_copy(source, target, small_sem.at[i])
        for i, (source, target) in enumerate(
            [(labels_hbm, labels_ref), (order_hbm, order_ref), (reg_hbm, reg_ref)]
        )
    ]
    for load in small:
        load.start()
    barrier = pltpu.get_barrier_semaphore()
    for peer in peers:
        pl.semaphore_signal(barrier, inc=1, device_id=peer, device_id_type=MESH)

    contract_last = (((1,), (1,)), ((), ()))
    gram = jnp.zeros((rows, rows), jnp.float32)
    for i, load in enumerate(loads):
        load.wait()
        block = data[:, pl.ds(i * width, width)]
        gram = gram + lax.dot_general(
            block, block, contract_last, preferred_element_type=jnp.float32
        )

    scale = 1.0 / math.sqrt(features)
    sigma = float(X * ZHI * CORE)
    reg_row = lax.broadcasted_iota(jnp.int32, (REGS, 1), 0)
    strength = 0.04 * jnp.exp(0.5 * math.log(2.0) * reg_row.astype(jnp.float32))
    total = strength * samples_all
    coupling = sigma * scale * scale / total

    def local_round(gram, signs, visit):
        n = gram.shape[0]
        row = lax.broadcasted_iota(jnp.int32, (n, n), 0)
        col = lax.broadcasted_iota(jnp.int32, (n, n), 1)
        diagonal = jnp.sum(jnp.where(row == col, gram, 0.0), axis=0, keepdims=True)
        gain = total / (sigma * (diagonal / features + 1e-6))
        high = gram.astype(jnp.bfloat16)
        low = (gram - high.astype(jnp.float32)).astype(jnp.bfloat16)

        def run(base, dual):
            full = jnp.zeros((REGS, n), jnp.float32)
            new_dual = dual
            for t in range(NBLOCKS):
                score = base
                if t:
                    coef = full.astype(jnp.bfloat16)
                    score = base + coupling * (
                        jnp.dot(coef, high, preferred_element_type=jnp.float32)
                        + jnp.dot(coef, low, preferred_element_type=jnp.float32)
                    )
                updated = jnp.clip(dual + gain * (1.0 - signs * score), 0.0, 1.0)
                step = (signs * (updated - dual)).astype(jnp.bfloat16).astype(jnp.float32)
                full = jnp.where(visit == t, step, full)
                new_dual = jnp.where(visit == t, updated, new_dual)
            return full, new_dual

        return run

    for load in small:
        load.wait()
    signs = labels_ref[...].astype(jnp.float32)
    block_of = lax.broadcasted_iota(jnp.int32, (1, rows), 1) // (rows // NBLOCKS)
    visit = jnp.zeros((1, rows), jnp.int32)
    for t in range(1, NBLOCKS):
        visit = jnp.where(block_of == order_ref[0, t], t, visit)
    zero = jnp.zeros((REGS, rows), jnp.float32)
    full, dual = local_round(gram, signs, visit)(zero, zero)

    slot = y * ZLO + part
    start = pl.multiple_of(slot * share, share)
    own = pl.ds(pl.multiple_of(mine * piece, piece), piece)
    pl.semaphore_wait(barrier, len(peers))

    def copy(source, target, sends, recvs, i, peer):
        return pltpu.make_async_remote_copy(
            src_ref=source,
            dst_ref=target,
            send_sem=sends.at[i],
            recv_sem=recvs.at[i],
            device_id=peer,
            device_id_type=MESH,
        )

    pending = []

    def to_plane(stage, make):
        copies = []
        for d in range(1, PLANE):
            other, peer = plane_peer(d)
            source, target = make(d, other)
            c = copy(source, target, plane_send, plane_recv, stage * (PLANE - 1) + d - 1, peer)
            c.start()
            copies.append(c)
        pending.extend(copies)
        return copies

    def to_cubes(stage, source, target):
        copies = []
        for d in range(1, ZHI):
            c = copy(source, target, cube_send, cube_recv, stage * (ZHI - 1) + d - 1, cube_peer(d))
            c.start()
            copies.append(c)
        pending.extend(copies)
        return copies

    def to_grp(stage, source, target):
        copies = []
        for d in range(1, GRP):
            c = copy(source, target, grp_send, grp_recv, stage * (GRP - 1) + d - 1, grp_peer(d))
            c.start()
            copies.append(c)
        pending.extend(copies)
        return copies

    def arrived(copies):
        for c in copies:
            c.wait_recv()

    def summed(ref, count):
        out = ref[0]
        for j in range(1, count):
            out = out + ref[j]
        return out

    delta[...] = (scale / total) * jnp.dot(
        full.astype(jnp.bfloat16), data[:, pl.ds(start, share)], preferred_element_type=jnp.float32
    )

    def scatter(d, other):
        where = pl.ds(pl.multiple_of(other * piece, piece), piece)
        return delta.at[:, where], sums1.at[d - 1]

    scattered = to_plane(0, scatter)
    for j in range(PLANE):
        where = pl.ds(pl.multiple_of(start + j * piece, piece), piece)
        wide[j] = data[:, where].astype(jnp.float32)

    per_half = LANES // rows
    lane = lax.broadcasted_iota(jnp.int32, (1, LANES), 1) // rows
    known = jnp.concatenate([signs, visit.astype(jnp.float32), dual], axis=0)
    known = jnp.concatenate([known] * per_half, axis=1)
    known = jnp.where(lane == lax.rem(mine, per_half), known, 0.0)
    packed = jnp.concatenate([gram[8 * i : 8 * i + 8] for i in range(per_half)], axis=1)
    known = jnp.concatenate([packed, known], axis=0)
    facts_own[...] = known
    facts[mine] = known
    across[mine] = data[:, pl.ds(pl.multiple_of(start + mine * piece, piece), piece)].astype(
        jnp.float32
    )

    notes = to_plane(1, lambda d, other: (facts_own, facts.at[mine]))
    pieces = to_plane(2, lambda d, other: (wide.at[other], across.at[mine]))

    for s in range(REACH - 1):
        pl.semaphore_signal(relay.at[0, s], inc=1, device_id=right, device_id_type=MESH)
        pl.semaphore_signal(relay.at[1, s], inc=1, device_id=left, device_id_type=MESH)
        pl.semaphore_wait(relay.at[0, s], 1)
        pl.semaphore_wait(relay.at[1, s], 1)

    arrived(scattered)
    step = delta[:, own] + summed(sums1, PLANE - 1)

    held = None
    for r in range(ROUNDS):
        part2[r] = step
        sums2[r, zhi] = step
        cubes = to_cubes(r, part2.at[r], sums2.at[r, zhi])
        if r == 0:
            arrived(notes)
            half = PLANE // 2
            low_half, high_half = facts[0, 8:], facts[half, 8:]
            for j in range(1, half):
                low_half = low_half + facts[j, 8:]
                high_half = high_half + facts[half + j, 8:]
            known = jnp.concatenate([low_half, high_half], axis=1)
            signs, visit, dual = known[0:1], known[1:2].astype(jnp.int32), known[2:]
            gram = []
            for j in range(PLANE):
                packed = facts[j, :8]
                parts = [packed[:, i * rows : (i + 1) * rows] for i in range(per_half)]
                one = [jnp.concatenate(parts, axis=0)]
                if j:
                    one = [jnp.zeros((rows, j * rows), jnp.float32)] + one
                if j + 1 < PLANE:
                    one = one + [jnp.zeros((rows, (PLANE - 1 - j) * rows), jnp.float32)]
                gram.append(jnp.concatenate(one, axis=1))
            gram = jnp.concatenate(gram, axis=0)
            solve = local_round(gram, signs, visit)
            arrived(pieces)
            block = across[...].reshape(wide_rows, piece).astype(jnp.bfloat16)
        arrived(cubes)
        step = summed(sums2.at[r], ZHI)
        held = step if held is None else held + step

        tile = scale * lax.dot_general(
            held.astype(jnp.bfloat16), block, contract_last, preferred_element_type=jnp.float32
        )
        last = r + 1 == ROUNDS
        if last:
            norm = jnp.sum(held * held, axis=1, keepdims=True)
            lanes = lax.broadcasted_iota(jnp.int32, (REGS, wide_rows), 1)
            norm = jnp.sum(jnp.where(lanes == reg_row, norm, 0.0), axis=0, keepdims=True)
            tile = jnp.concatenate([tile, norm], axis=0)
        own3, all3, own4, all4 = (
            (last3, last_sums3, last4, last_sums4) if last else (local3, sums3, local4, sums4)
        )
        own3[...] = tile
        all3[mine] = tile
        arrived(to_plane(3 + r, lambda d, other: (own3, all3.at[mine])))
        tile = summed(all3, PLANE)
        own4[...] = tile
        all4[slot] = tile
        arrived(to_grp(r, own4, all4.at[slot]))
        tile = summed(all4, GRP)
        margins = tile[:REGS]
        if not last:
            full, dual = solve(margins, dual)
            step = (scale / total) * jnp.dot(
                full.astype(jnp.bfloat16), block, preferred_element_type=jnp.float32
            )

    hinge = jnp.maximum(0.0, 1.0 - signs * margins)
    cube_total = jnp.broadcast_to(jnp.sum(hinge - dual, axis=1, keepdims=True), (REGS, LANES))
    local5[...] = cube_total
    sums5[zhi] = cube_total
    cubes = to_cubes(ROUNDS, local5, sums5.at[zhi])

    chosen = reg_row == reg_ref[0, 0]

    def own_rows(values):
        values = jnp.sum(jnp.where(chosen, values, 0.0), axis=0, keepdims=True)
        out = jnp.zeros((1, rows), jnp.float32)
        for j in range(PLANE):
            out = out + jnp.where(mine == j, values[:, j * rows : (j + 1) * rows], 0.0)
        return out

    own_dual, own_margins = own_rows(dual), own_rows(margins)
    norm = jnp.sum(
        jnp.where(lax.broadcasted_iota(jnp.int32, (1, wide_rows), 1) == reg_ref[0, 0], tile[REGS:], 0.0),
        axis=1,
        keepdims=True,
    )
    arrived(cubes)
    everyone = summed(sums5, ZHI)[:, :1]
    gap = jnp.sum(jnp.where(chosen, everyone / samples_all, 0.0), axis=0, keepdims=True)
    gap = gap + norm * jnp.sum(jnp.where(chosen, strength, 0.0), axis=0, keepdims=True)
    rest = LANES - 2 * rows
    out[...] = jnp.concatenate([own_dual, own_margins, jnp.broadcast_to(gap, (1, rest))], axis=1)
    for c in pending:
        c.wait_send()


def shards(data, labels, order, reg_index):
    rows, features = data.shape
    share = features // GRP
    piece = share // PLANE
    chunks = 8
    f32 = functools.partial(jax.ShapeDtypeStruct, dtype=jnp.float32)
    vmem = pl.BlockSpec(memory_space=pltpu.VMEM)
    scratch = lambda *shape: pltpu.VMEM(shape, jnp.float32)
    sems = lambda n: pltpu.SemaphoreType.DMA((n,))
    wide_rows = PLANE * rows
    known = 8 + 2 + REGS
    out = pl.pallas_call(
        functools.partial(kernel, rows * lax.axis_size("blk"), chunks),
        out_shape=f32((1, LANES)),
        in_specs=[pl.BlockSpec(memory_space=pl.ANY)] * 4,
        out_specs=vmem,
        scratch_shapes=[
            pltpu.VMEM((1, rows), jnp.int32),
            pltpu.SMEM((1, NBLOCKS), jnp.int32),
            pltpu.SMEM((1, 1), jnp.int32),
            sems(3),
            pltpu.VMEM((rows, features), jnp.bfloat16),
            sems(chunks),
            scratch(REGS, share),
            scratch(PLANE - 1, REGS, piece),
            scratch(ROUNDS, REGS, piece),
            scratch(ROUNDS, ZHI, REGS, piece),
            scratch(PLANE, rows, piece),
            scratch(PLANE, rows, piece),
            scratch(known, LANES),
            scratch(PLANE, known, LANES),
            scratch(REGS, wide_rows),
            scratch(PLANE, REGS, wide_rows),
            scratch(REGS, wide_rows),
            scratch(GRP, REGS, wide_rows),
            scratch(REGS + 1, wide_rows),
            scratch(PLANE, REGS + 1, wide_rows),
            scratch(REGS + 1, wide_rows),
            scratch(GRP, REGS + 1, wide_rows),
            scratch(REGS, LANES),
            scratch(ZHI, REGS, LANES),
            sems((3 + ROUNDS) * (PLANE - 1)),
            sems((3 + ROUNDS) * (PLANE - 1)),
            sems((ROUNDS + 1) * (ZHI - 1)),
            sems((ROUNDS + 1) * (ZHI - 1)),
            sems(ROUNDS * (GRP - 1)),
            sems(ROUNDS * (GRP - 1)),
            pltpu.SemaphoreType.REGULAR((2, REACH - 1)),
        ],
        compiler_params=pltpu.CompilerParams(collective_id=0, has_side_effects=True),
    )(labels.reshape(1, rows), order, reg_index.reshape(1, 1), data)
    out = out.reshape(LANES)
    return out[:rows], out[rows : 2 * rows], out[2 * rows : 2 * rows + 1]


def solution(mesh):
    placed = (P("blk", None), P("blk"), P("blk", None), P("grp"))
    return jax.shard_map(
        shards,
        mesh=mesh,
        in_specs=placed,
        out_specs=(P(("grp", "blk")), P(("grp", "blk")), P("grp")),
        check_vma=False,
    )
```

time: 74.5 us -> 68.9 us (0.925)
  Pallas kernels: 69 us -> 64.9 us
  between operations: 3.05 us -> 1.29 us
    pallas_call x1, Pallas kernels: 69 us -> 64.9 us  [shards(): pl.pallas_call(functools.partial(kernel, rows * lax.axis_size('blk'), chu...]
    slice x0 -> x2, local copies, waits for them, and re-layouts: none -> 2.43 us  [shards(): return (out[:rows], out[rows:2 * rows], out[2 * rows:2 * rows + 1])]
    unnamed x2 -> x0, local copies, waits for them, and re-layouts: 2.25 us -> none
where the time goes in v2:
time: 68.9 us; the launch traced here: 68.6 us
  Pallas kernels  64.9 us (94%)
  local copies, waits for them, and re-layouts  2.43 us (4%)
  between operations  1.29 us (2%)
    pallas_call x1, Pallas kernels, shards(): pl.pallas_call(functools.partial(kernel, rows * lax.axis_size('blk'), chu...  64.9 us
    slice x2, local copies, waits for them, and re-layouts, shards(): return (out[:rows], out[rows:2 * rows], out[2 * rows:2 * rows + 1])  2.43 us

profile of v2, /device:TPU:1, one launch (start us, length us, event | category | flops | bytes accessed | tf_op | source)
XLA Modules:
  0.0 68.6 jit_solution(9155239566577917807)
XLA Ops:
  1.3 64.9 %shard_map.67 = f32[1,128]{1,0:T(1,128)} custom-call(s32[1,32]{1,0:T(1,128)} %bitcast.8, s32[1,4]{1,0:T(1,128)} %order_hbm.1, s32[1,1]{1,0:T(1,128)} %bitcast.7.reg_hbm, bf16[32,65536]{1,0:T(8,128)(2,1)} %data_hbm.1), custom_call_target="tpu_custom_call" | custom-call | tf_op jit(solution)/shard_map/pallas_call | solution.py:366
  66.2 1.3 %slice_bitcast_fusion = (f32[32]{0:T(128)}, f32[32]{0:T(128)}) fusion(f32[1,128]{1,0:T(1,128)} %shard_map.67), kind=kLoop, calls=%fused_computation | loop fusion | bytes 512 | tf_op jit(solution)/shard_map/slice | solution.py:407
  67.4 1.2 %slice.22 = f32[1,1]{1,0:T(1,128)} slice(f32[1,128]{1,0:T(1,128)} %shard_map.67), slice={[0:1], [64:65]} | slice | bytes 8 | tf_op jit(solution)/shard_map/slice | solution.py:407

commit v3 on v2

--- a/solution.py
+++ b/solution.py
@@ -16,7 +16,6 @@
 PLANE = X * CORE
 GRP = Y * ZLO
 LANES = 128
-REACH = 6
 MESH = pl.DeviceIdType.MESH
 
 
@@ -58,7 +57,6 @@
     cube_recv,
     grp_send,
     grp_recv,
-    relay,
 ):
     rows, features = data.shape
     share = features // GRP
@@ -82,15 +80,9 @@
     def grp_peer(d):
         return (lax.rem(grp + d, GRP), blk)
 
-    def z_peer(d):
-        z = lax.rem(zhi * ZLO + zlo + d + ZHI * ZLO, ZHI * ZLO)
-        return (y * ZLO + lax.rem(z, ZLO), x * ZHI * CORE + (z // ZLO) * CORE + core)
-
-    left, right = z_peer(-1), z_peer(1)
-    peers = [plane_peer(d)[1] for d in range(1, PLANE)]
-    peers += [(lax.rem(grp + d * ZLO, GRP), blk) for d in range(1, Y)]
-    peers += [left, right]
-
+    peers = [cube_peer(d) for d in (2, 1, 3)]
+    peers += [grp_peer(d) for d in range(1, GRP)]
+    peers += [plane_peer(d)[1] for d in range(1, PLANE)]
     width = features // chunks
     loads = [
         pltpu.make_async_copy(
@@ -171,7 +163,6 @@
     slot = y * ZLO + part
     start = pl.multiple_of(slot * share, share)
     own = pl.ds(pl.multiple_of(mine * piece, piece), piece)
-    pl.semaphore_wait(barrier, len(peers))
 
     def copy(source, target, sends, recvs, i, peer):
         return pltpu.make_async_remote_copy(
@@ -227,6 +218,8 @@
     delta[...] = (scale / total) * jnp.dot(
         full.astype(jnp.bfloat16), data[:, pl.ds(start, share)], preferred_element_type=jnp.float32
     )
+
+    pl.semaphore_wait(barrier, len(peers))
 
     def scatter(d, other):
         where = pl.ds(pl.multiple_of(other * piece, piece), piece)
@@ -252,12 +245,6 @@
 
     notes = to_plane(1, lambda d, other: (facts_own, facts.at[mine]))
     pieces = to_plane(2, lambda d, other: (wide.at[other], across.at[mine]))
-
-    for s in range(REACH - 1):
-        pl.semaphore_signal(relay.at[0, s], inc=1, device_id=right, device_id_type=MESH)
-        pl.semaphore_signal(relay.at[1, s], inc=1, device_id=left, device_id_type=MESH)
-        pl.semaphore_wait(relay.at[0, s], 1)
-        pl.semaphore_wait(relay.at[1, s], 1)
 
     arrived(scattered)
     step = delta[:, own] + summed(sums1, PLANE - 1)
@@ -399,7 +386,6 @@
             sems((ROUNDS + 1) * (ZHI - 1)),
             sems(ROUNDS * (GRP - 1)),
             sems(ROUNDS * (GRP - 1)),
-            pltpu.SemaphoreType.REGULAR((2, REACH - 1)),
         ],
         compiler_params=pltpu.CompilerParams(collective_id=0, has_side_effects=True),
     )(labels.reshape(1, rows), order, reg_index.reshape(1, 1), data)

time: 68.9 us -> 67 us (0.972)
  Pallas kernels: 64.9 us -> 63 us
    pallas_call x1, Pallas kernels: 64.9 us -> 63 us  [shards(): pl.pallas_call(functools.partial(kernel, rows * lax.axis_size('blk'), chu...]
where the time goes in v3:
time: 67 us; the launch traced here: 66.7 us
  Pallas kernels  63 us (94%)
  local copies, waits for them, and re-layouts  2.43 us (4%)
  between operations  1.29 us (2%)
    pallas_call x1, Pallas kernels, shards(): pl.pallas_call(functools.partial(kernel, rows * lax.axis_size('blk'), chu...  63 us
    slice x2, local copies, waits for them, and re-layouts, shards(): return (out[:rows], out[rows:2 * rows], out[2 * rows:2 * rows + 1])  2.43 us

profile of v3, /device:TPU:1, one launch (start us, length us, event | category | flops | bytes accessed | tf_op | source)
XLA Modules:
  0.0 66.7 jit_solution(7739703967872063888)
XLA Ops:
  1.3 63.0 %shard_map.67 = f32[1,128]{1,0:T(1,128)} custom-call(s32[1,32]{1,0:T(1,128)} %bitcast.8, s32[1,4]{1,0:T(1,128)} %order_hbm.1, s32[1,1]{1,0:T(1,128)} %bitcast.7.reg_hbm, bf16[32,65536]{1,0:T(8,128)(2,1)} %data_hbm.1), custom_call_target="tpu_custom_call" | custom-call | tf_op jit(solution)/shard_map/pallas_call | solution.py:353
  64.3 1.3 %slice_bitcast_fusion = (f32[32]{0:T(128)}, f32[32]{0:T(128)}) fusion(f32[1,128]{1,0:T(1,128)} %shard_map.67), kind=kLoop, calls=%fused_computation | loop fusion | bytes 512 | tf_op jit(solution)/shard_map/slice | solution.py:393
  65.6 1.2 %slice.22 = f32[1,1]{1,0:T(1,128)} slice(f32[1,128]{1,0:T(1,128)} %shard_map.67), slice={[0:1], [64:65]} | slice | bytes 8 | tf_op jit(solution)/shard_map/slice | solution.py:393

commit v4 on v3

--- a/solution.py
+++ b/solution.py
@@ -59,6 +59,25 @@
     grp_recv,
 ):
     rows, features = data.shape
+    width = features // chunks
+    loads = [
+        pltpu.make_async_copy(
+            data_hbm.at[:, pl.ds(i * width, width)],
+            data.at[:, pl.ds(i * width, width)],
+            load_sem.at[i],
+        )
+        for i in range(chunks)
+    ]
+    for load in loads:
+        load.start()
+    small = [
+        pltpu.make_async_copy(source, target, small_sem.at[i])
+        for i, (source, target) in enumerate(
+            [(labels_hbm, labels_ref), (order_hbm, order_ref), (reg_hbm, reg_ref)]
+        )
+    ]
+    for load in small:
+        load.start()
     share = features // GRP
     piece = share // PLANE
     wide_rows = PLANE * rows
@@ -83,25 +102,6 @@
     peers = [cube_peer(d) for d in (2, 1, 3)]
     peers += [grp_peer(d) for d in range(1, GRP)]
     peers += [plane_peer(d)[1] for d in range(1, PLANE)]
-    width = features // chunks
-    loads = [
-        pltpu.make_async_copy(
-            data_hbm.at[:, pl.ds(i * width, width)],
-            data.at[:, pl.ds(i * width, width)],
-            load_sem.at[i],
-        )
-        for i in range(chunks)
-    ]
-    for load in loads:
-        load.start()
-    small = [
-        pltpu.make_async_copy(source, target, small_sem.at[i])
-        for i, (source, target) in enumerate(
-            [(labels_hbm, labels_ref), (order_hbm, order_ref), (reg_hbm, reg_ref)]
-        )
-    ]
-    for load in small:
-        load.start()
     barrier = pltpu.get_barrier_semaphore()
     for peer in peers:
         pl.semaphore_signal(barrier, inc=1, device_id=peer, device_id_type=MESH)
@@ -314,7 +314,7 @@
     sums5[zhi] = cube_total
     cubes = to_cubes(ROUNDS, local5, sums5.at[zhi])
 
-    chosen = reg_row == reg_ref[0, 0]
+    chosen = reg_row == reg_ref[0]
 
     def own_rows(values):
         values = jnp.sum(jnp.where(chosen, values, 0.0), axis=0, keepdims=True)
@@ -325,7 +325,7 @@
 
     own_dual, own_margins = own_rows(dual), own_rows(margins)
     norm = jnp.sum(
-        jnp.where(lax.broadcasted_iota(jnp.int32, (1, wide_rows), 1) == reg_ref[0, 0], tile[REGS:], 0.0),
+        jnp.where(lax.broadcasted_iota(jnp.int32, (1, wide_rows), 1) == reg_ref[0], tile[REGS:], 0.0),
         axis=1,
         keepdims=True,
     )
@@ -337,6 +337,13 @@
     out[...] = jnp.concatenate([own_dual, own_margins, jnp.broadcast_to(gap, (1, rest))], axis=1)
     for c in pending:
         c.wait_send()
+
+
+def handed_out(out, dual, margins, gap):
+    rows = dual.shape[1]
+    dual[...] = out[:, :rows]
+    margins[...] = out[:, rows : 2 * rows]
+    gap[...] = out[:, 2 * rows : 2 * rows + 1]
 
 
 def shards(data, labels, order, reg_index):
@@ -352,13 +359,13 @@
     known = 8 + 2 + REGS
     out = pl.pallas_call(
         functools.partial(kernel, rows * lax.axis_size("blk"), chunks),
-        out_shape=f32((1, LANES)),
+        out_shape=pltpu.VMEM((1, LANES), jnp.float32),
         in_specs=[pl.BlockSpec(memory_space=pl.ANY)] * 4,
         out_specs=vmem,
         scratch_shapes=[
             pltpu.VMEM((1, rows), jnp.int32),
             pltpu.SMEM((1, NBLOCKS), jnp.int32),
-            pltpu.SMEM((1, 1), jnp.int32),
+            pltpu.SMEM((1,), jnp.int32),
             sems(3),
             pltpu.VMEM((rows, features), jnp.bfloat16),
             sems(chunks),
@@ -388,9 +395,16 @@
             sems(ROUNDS * (GRP - 1)),
         ],
         compiler_params=pltpu.CompilerParams(collective_id=0, has_side_effects=True),
-    )(labels.reshape(1, rows), order, reg_index.reshape(1, 1), data)
-    out = out.reshape(LANES)
-    return out[:rows], out[rows : 2 * rows], out[2 * rows : 2 * rows + 1]
+    )(labels.reshape(1, rows), order, reg_index, data)
+    return tuple(
+        a.reshape(-1)
+        for a in pl.pallas_call(
+            handed_out,
+            out_shape=(f32((1, rows)), f32((1, rows)), f32((1, 1))),
+            in_specs=[vmem],
+            out_specs=(vmem, vmem, vmem),
+        )(pltpu.with_memory_space_constraint(out, pltpu.VMEM))
+    )
 
 
 def solution(mesh):

time: 67 us -> 64.5 us (0.963)
  local copies, waits for them, and re-layouts: 2.43 us -> 0 us
    slice x2 -> x0, local copies, waits for them, and re-layouts: 2.43 us -> none  [shards(): return (out[:rows], out[rows:2 * rows], out[2 * rows:2 * rows + 1])]
where the time goes in v4:
time: 64.5 us; the launch traced here: 64.2 us
  Pallas kernels  63 us (98%)
  between operations  1.29 us (2%)
    pallas_call x1, Pallas kernels, shards(): pl.pallas_call(functools.partial(kernel, rows * lax.axis_size('blk'), chu...  62.4 us

profile of v4, /device:TPU:1, one launch (start us, length us, event | category | flops | bytes accessed | tf_op | source)
XLA Modules:
  0.0 64.2 jit_solution(5579490374496138700)
XLA Ops:
  1.3 62.4 %shard_map.67.out = f32[1,128]{1,0:T(1,128)S(1)} custom-call(s32[1,32]{1,0:T(1,128)} %bitcast.4, s32[1,4]{1,0:T(1,128)} %order_hbm.1, s32[1]{0:T(128)S(6)} %copy.7.reg_hbm, bf16[32,65536]{1,0:T(8,128)(2,1)} %data_hbm.1), custom_call_target="tpu_custom_call" | custom-call | tf_op jit(solution)/shard_map/pallas_call | solution.py:360
  63.7 0.6 shard_map.68

commit v5 on v4

--- a/solution.py
+++ b/solution.py
@@ -178,7 +178,7 @@
 
     def to_plane(stage, make):
         copies = []
-        for d in range(1, PLANE):
+        for d in (4, 3, 5, 2, 6, 1, 7):
             other, peer = plane_peer(d)
             source, target = make(d, other)
             c = copy(source, target, plane_send, plane_recv, stage * (PLANE - 1) + d - 1, peer)
@@ -189,7 +189,7 @@
 
     def to_cubes(stage, source, target):
         copies = []
-        for d in range(1, ZHI):
+        for d in (2, 1, 3):
             c = copy(source, target, cube_send, cube_recv, stage * (ZHI - 1) + d - 1, cube_peer(d))
             c.start()
             copies.append(c)
@@ -198,7 +198,7 @@
 
     def to_grp(stage, source, target):
         copies = []
-        for d in range(1, GRP):
+        for d in (8, 7, 9, 6, 10, 5, 11, 4, 12, 3, 13, 2, 14, 1, 15):
             c = copy(source, target, grp_send, grp_recv, stage * (GRP - 1) + d - 1, grp_peer(d))
             c.start()
             copies.append(c)

time: 64.5 us -> 62.5 us (0.969)
  Pallas kernels: 63 us -> 61.1 us
    pallas_call x1, Pallas kernels: 62.4 us -> 60.5 us  [shards(): pl.pallas_call(functools.partial(kernel, rows * lax.axis_size('blk'), chu...]
where the time goes in v5:
time: 62.5 us; the launch traced here: 62.4 us
  Pallas kernels  61.1 us (98%)
  between operations  1.29 us (2%)
    pallas_call x1, Pallas kernels, shards(): pl.pallas_call(functools.partial(kernel, rows * lax.axis_size('blk'), chu...  60.5 us

profile of v5, /device:TPU:1, one launch (start us, length us, event | category | flops | bytes accessed | tf_op | source)
XLA Modules:
  0.0 62.4 jit_solution(17756757356205237091)
XLA Ops:
  1.3 60.5 %shard_map.67.out = f32[1,128]{1,0:T(1,128)S(1)} custom-call(s32[1,32]{1,0:T(1,128)} %bitcast.4, s32[1,4]{1,0:T(1,128)} %order_hbm.1, s32[1]{0:T(128)S(6)} %copy.7.reg_hbm, bf16[32,65536]{1,0:T(8,128)(2,1)} %data_hbm.1), custom_call_target="tpu_custom_call" | custom-call | tf_op jit(solution)/shard_map/pallas_call | solution.py:360
  61.8 0.6 shard_map.68

commit v6 on v5

--- a/solution.py
+++ b/solution.py
@@ -244,7 +244,6 @@
     )
 
     notes = to_plane(1, lambda d, other: (facts_own, facts.at[mine]))
-    pieces = to_plane(2, lambda d, other: (wide.at[other], across.at[mine]))
 
     arrived(scattered)
     step = delta[:, own] + summed(sums1, PLANE - 1)
@@ -255,6 +254,7 @@
         sums2[r, zhi] = step
         cubes = to_cubes(r, part2.at[r], sums2.at[r, zhi])
         if r == 0:
+            pieces = to_plane(2, lambda d, other: (wide.at[other], across.at[mine]))
             arrived(notes)
             half = PLANE // 2
             low_half, high_half = facts[0, 8:], facts[half, 8:]

time: 62.5 us -> 63.3 us (1.013)
  no operation moved by 1% of the time
where the time goes in v6:
time: 63.3 us; the launch traced here: 62.9 us
  Pallas kernels  61.6 us (97%)
  between operations  1.29 us (2%)
    pallas_call x1, Pallas kernels, shards(): pl.pallas_call(functools.partial(kernel, rows * lax.axis_size('blk'), chu...  61 us

profile of v6, /device:TPU:1, one launch (start us, length us, event | category | flops | bytes accessed | tf_op | source)
XLA Modules:
  0.0 62.9 jit_solution(423920910802814640)
XLA Ops:
  1.3 61.0 %shard_map.67.out = f32[1,128]{1,0:T(1,128)S(1)} custom-call(s32[1,32]{1,0:T(1,128)} %bitcast.4, s32[1,4]{1,0:T(1,128)} %order_hbm.1, s32[1]{0:T(128)S(6)} %copy.7.reg_hbm, bf16[32,65536]{1,0:T(8,128)(2,1)} %data_hbm.1), custom_call_target="tpu_custom_call" | custom-call | tf_op jit(solution)/shard_map/pallas_call | solution.py:360
  62.3 0.6 shard_map.68
